TPU v7x, 256 devices: a whole 4x4x8 slice. The times are simulated.
256 devices in a mesh: bead: 8 (over y_lo, x), dom: 32 (over y_hi, z, core).
Axes of the slice: x: 4, y: 4 (y_hi: 2, y_lo: 2; y = y_hi * 2 + y_lo), z: 8, core: 2. Of those that a mesh axis runs over, the one named last changes fastest.
Arguments:
- mode_pos: float32 [16, 3, 24576], P('bead', None, 'dom'), may hold values from -6 to 6
- mode_vel: float32 [16, 3, 24576], P('bead', None, 'dom'), may hold values from -6 to 6
- charges: float32 [24576], P('dom'), may hold values from -1.5 to 1.5
Outputs:
- positions: float32 [16, 3, 24576], P('bead', None, 'dom')
- velocities: float32 [16, 3, 24576], P('bead', None, 'dom')
All inputs are finite; a program needn't handle non-finite values.
Results may differ from a plain program's by a relative error of at most 0.0003.
Values sent between devices are 32-bit elements; how exact they have to be, the bound alone decides.
No kernel may reach another device: no remote copies, remote signals or barrier semaphores. Data moves between devices by JAX's collectives and lax.ppermute only.
A program may use at most 64 MiB of HBM per device.

v0:
```python
import jax
import jax.numpy as jnp
from jax import lax
from jax.sharding import PartitionSpec as P

BEADS = 16
KAPPA = 2.0
SOFTEN = 0.09
KICK = 0.3
OMEGA = 7.0
STEP_TIME = 0.1
HIGHEST = lax.Precision.HIGHEST


def mode_table(bead_index, mode_index):
    scale_root = jnp.sqrt(jnp.float32(BEADS))
    angle = 2.0 * jnp.pi * bead_index.astype(jnp.float32) * mode_index.astype(jnp.float32) / BEADS
    first = jnp.ones_like(angle) / scale_root
    middle = jnp.cos(jnp.pi * bead_index.astype(jnp.float32)) / scale_root + 0.0 * angle
    factor = jnp.sqrt(2.0 / jnp.float32(BEADS))
    return jnp.where(
        mode_index == 0,
        first,
        jnp.where(
            2 * mode_index < BEADS,
            factor * jnp.cos(angle),
            jnp.where(2 * mode_index == BEADS, middle, factor * jnp.sin(angle)),
        ),
    )


def evolve(mode_pos, mode_vel, mode_index):
    freq = 2.0 * OMEGA * jnp.sin(jnp.pi * mode_index.astype(jnp.float32) / BEADS)
    theta = freq * STEP_TIME
    cosine = jnp.cos(theta)[:, None, None]
    sine = jnp.sin(theta)
    safe_freq = jnp.where(mode_index > 0, freq, 1.0)
    carry_rate = jnp.where(mode_index > 0, sine / safe_freq, STEP_TIME)[:, None, None]
    new_pos = cosine * mode_pos + carry_rate * mode_vel
    new_vel = (-freq * sine)[:, None, None] * mode_pos + cosine * mode_vel
    return (new_pos, new_vel)


def pair_block(near_pos, near_charge, far_pack):
    far_pos = far_pack[:, :3]
    far_charge = far_pack[:, 3]
    delta = near_pos[:, :, :, None] - far_pos[:, :, None, :]
    square = jnp.sum(delta * delta, axis=1) + SOFTEN
    distance = jnp.sqrt(square)
    weight = (
        near_charge[None, :, None]
        * far_charge[:, None, :]
        * jnp.exp(-KAPPA * distance)
        * (1.0 + KAPPA * distance)
        / (square * distance)
    )
    terms = weight[:, None] * delta
    return (jnp.sum(terms, axis=3), -jnp.sum(terms, axis=2))


def block_force(near_pos, near_charge, far_pack):
    far_count = far_pack.shape[2]
    span_size = far_count
    while span_size > 512 and span_size % 2 == 0:
        span_size = span_size // 2

    def one_span(total, span_index):
        piece = lax.dynamic_slice_in_dim(far_pack, span_index * span_size, span_size, 2)
        force_part, react_part = pair_block(near_pos, near_charge, piece)
        return (total + force_part, None)

    total, reacts = lax.scan(
        one_span, jnp.zeros_like(near_pos), jnp.arange(far_count // span_size, dtype=jnp.int32)
    )
    return (total, reacts)


def local(mode_pos, mode_vel, charges):
    local_beads = mode_pos.shape[0]
    own_modes = lax.axis_index("bead") * local_beads + jnp.arange(local_beads, dtype=jnp.int32)
    new_pos, new_vel = evolve(mode_pos, mode_vel, own_modes)
    pieces = (
        lax.all_gather(new_pos, "bead", axis=0, tiled=True),
        lax.all_gather(new_vel, "bead", axis=0, tiled=True),
    )
    span_count = pieces[0].shape[0]
    columns = jnp.arange(span_count, dtype=jnp.int32)
    table = mode_table(own_modes[:, None], columns[None, :])
    first = jnp.einsum("bk,kcn->bcn", table, pieces[0], precision=HIGHEST)
    second = jnp.einsum("bk,kcn->bcn", table, pieces[1], precision=HIGHEST)
    charge_rows = jnp.broadcast_to(charges[None, None, :], (local_beads, 1, charges.shape[0]))
    packed = jnp.concatenate((first, charge_rows), axis=1)
    force_part, unused = block_force(
        first, charges, lax.all_gather(packed, "dom", axis=2, tiled=True)
    )
    return (first, second + KICK * force_part)


def solution(mesh):
    placed = (P("bead", None, "dom"), P("bead", None, "dom"), P("dom"))
    return jax.shard_map(
        local,
        mesh=mesh,
        in_specs=placed,
        out_specs=(P("bead", None, "dom"), P("bead", None, "dom")),
        check_vma=False,
    )
```

profile of v0, /device:TPU:6, one launch (start us, length us, event | category | flops | bytes accessed | tf_op | source)
XLA Modules:
  0.0 468.5 jit_solution(9863614057664356881)
XLA Ops:
  1.6 28.3 %all_gather.9 = f32[16,3,768]{2,1,0:T(4,128)S(1)} all-gather(f32[2,3,768]{2,1,0:T(4,128)S(1)} %get-tuple-element.87), channel_id=1, replica_groups=mesh['bead'=8,'dom'=32] {'bead'}, dimensions={0}, use_global_device_ids=true | all-gather | bytes 165888 | tf_op jit(solution)/shard_map/all_gather | solution.py:83
  31.0 47.0 %all_gather.11 = f32[2,4,24576]{2,0,1:T(2,128)S(1)} all-gather(f32[2,4,768]{2,0,1:T(2,128)S(1)} %pad_maximum_fusion), channel_id=1, replica_groups=mesh['bead'=8,'dom'=32] {'dom'}, dimensions={2}, use_global_device_ids=true | all-gather | bytes 811008 | tf_op jit(solution)/shard_map/all_gather | solution.py:94
  78.1 361.2 %while.11 = (s32[]{:T(128)}, f32[2,3,768]{2,1,0:T(4,128)S(1)}, f32[768]{0:T(1024)}, s32[64]{0:T(128)S(1)}, f32[2,4,24576]{2,0,1:T(2,128)S(1)}, /*index=5*/f32[2,...) while((s32[]{:T(128)}, f32[2,3,768]{2,1,0:T(4,128)S(1)}, ...), condition=%wide.region_3.4_spmd.clone, body=%wide.region_0.3_spmd.clone.sunk | while | flops 15340040 | bytes 9627877 | solution.py:72
  80.5 1.7 fusion.30
  86.1 1.7 fusion.30
  103.0 1.7 fusion.30
  108.7 1.7 fusion.30
  114.3 1.7 fusion.30
  125.6 1.7 fusion.30
  131.3 1.7 fusion.30
  136.9 1.7 fusion.30
  142.5 1.7 fusion.30
  153.8 1.7 fusion.30
  159.5 1.7 fusion.30
  165.1 1.7 fusion.30
  170.8 1.7 fusion.30
  182.0 1.7 fusion.30
  187.7 1.7 fusion.30
  193.3 1.7 fusion.30
  210.3 1.7 fusion.30
  215.9 1.7 fusion.30
  221.6 1.7 fusion.30
  232.8 1.7 fusion.30
  238.5 1.7 fusion.30
  244.1 1.7 fusion.30
  249.8 1.7 fusion.30
  261.1 1.7 fusion.30
  266.7 1.7 fusion.30
  272.3 1.7 fusion.30
  278.0 1.7 fusion.30
  289.3 1.7 fusion.30
  294.9 1.7 fusion.30
  300.6 1.7 fusion.30
  317.5 1.7 fusion.30
  323.1 1.7 fusion.30
  328.8 1.7 fusion.30
  340.1 1.7 fusion.30
  345.7 1.7 fusion.30
  351.4 1.7 fusion.30
  357.0 1.7 fusion.30
  368.3 1.7 fusion.30
  373.9 1.7 fusion.30
  379.6 1.7 fusion.30
  385.2 1.7 fusion.30
  396.5 1.7 fusion.30
  402.2 1.7 fusion.30
  407.8 1.7 fusion.30
  439.3 28.3 %all_gather.10 = f32[16,3,768]{2,1,0:T(4,128)S(1)} all-gather(f32[2,3,768]{2,1,0:T(4,128)S(1)} %get-tuple-element.86), channel_id=1, replica_groups=mesh['bead'=8,'dom'=32] {'bead'}, dimensions={0}, use_global_device_ids=true | all-gather | bytes 165888 | tf_op jit(solution)/shard_map/all_gather | solution.py:84
  (612 shorter events, 243.4 us)
Async XLA Ops:
  30.3 47.8 %copy-start = (f32[2,3,768]{2,0,1:T(2,128)}, f32[2,3,768]{2,0,1:T(2,128)S(1)}, u32[]{:S(2)}) copy-start(f32[2,3,768]{2,0,1:T(2,128)S(1)} %fusion.8) | copy-start | bytes 55300
  78.1 2.4 copy-start.1
  83.7 2.4 copy-start.1
  89.4 2.4 copy-start.1
  95.0 2.4 copy-start.1
  100.7 2.4 copy-start.1
  106.3 2.4 copy-start.1
  112.0 2.4 copy-start.1
  117.6 2.4 copy-start.1
  123.2 2.4 copy-start.1
  128.9 2.4 copy-start.1
  134.5 2.4 copy-start.1
  140.2 2.4 copy-start.1
  145.8 2.4 copy-start.1
  151.5 2.4 copy-start.1
  157.1 2.4 copy-start.1
  162.7 2.4 copy-start.1
  168.4 2.4 copy-start.1
  174.0 2.4 copy-start.1
  179.7 2.4 copy-start.1
  185.3 2.4 copy-start.1
  191.0 2.4 copy-start.1
  196.6 2.4 copy-start.1
  202.3 2.4 copy-start.1
  207.9 2.4 copy-start.1
  213.5 2.4 copy-start.1
  219.2 2.4 copy-start.1
  224.8 2.4 copy-start.1
  230.5 2.4 copy-start.1
  236.1 2.4 copy-start.1
  241.8 2.4 copy-start.1
  247.4 2.4 copy-start.1
  253.0 2.4 copy-start.1
  258.7 2.4 copy-start.1
  264.3 2.4 copy-start.1
  270.0 2.4 copy-start.1
  275.6 2.4 copy-start.1
  281.3 2.4 copy-start.1
  298.2 2.4 copy-start.1
  303.8 2.4 copy-start.1
  326.4 2.4 copy-start.1
  332.1 2.4 copy-start.1
  354.6 2.4 copy-start.1
  377.2 2.4 copy-start.1
  382.9 2.4 copy-start.1
  405.4 2.4 copy-start.1
  411.1 2.4 copy-start.1
  433.6 2.4 copy-start.1
  (17 other events, 40.1 us)
where the time goes:
time: 469 us; the launch traced here: 468 us
  other arithmetic  274 us (58%)
  blocking collectives  104 us (22%)
  loops' own time  46.5 us (10%)
  local copies, waits for them, and re-layouts  42.1 us (9%)
    div x64, other arithmetic, pair_block(): near_charge[None, :, None] * far_charge[:, None, :]  108 us
    reduce_sum x64, other arithmetic, pair_block(): return (jnp.sum(terms, axis=3), -jnp.sum(terms, axis=2))  98.3 us
    reduce_sum x64, other arithmetic, pair_block(): square = jnp.sum(delta * delta, axis=1) + SOFTEN  65.7 us
    all_gather x1, blocking collectives, local(): lax.all_gather(packed, 'dom', axis=2, tiled=True)  47 us
    another operation x1, loops' own time, block_force(): lax.scan(one_span, jnp.zeros_like(near_pos), jnp.arange(far_count // span...  46.5 us
    dynamic_slice x64, local copies, waits for them, and re-layouts, block_force(): lax.scan(one_span, jnp.zeros_like(near_pos), jnp.arange(far_count // span...  39.2 us
    all_gather x1, blocking collectives, local(): lax.all_gather(new_vel, 'bead', axis=0, tiled=True)  28.3 us
    all_gather x1, blocking collectives, local(): lax.all_gather(new_pos, 'bead', axis=0, tiled=True)  28.3 us

commit v1 on v0

--- a/solution.py
+++ b/solution.py
@@ -10,6 +10,11 @@
 OMEGA = 7.0
 STEP_TIME = 0.1
 HIGHEST = lax.Precision.HIGHEST
+
+
+def gather_over(x, mesh_axis, along):
+    sent = jnp.stack([x] * lax.axis_size(mesh_axis))
+    return jnp.concatenate(lax.all_to_all(sent, mesh_axis, 0, 0), axis=along)
 
 
 def mode_table(bead_index, mode_index):
@@ -90,9 +95,7 @@
     second = jnp.einsum("bk,kcn->bcn", table, pieces[1], precision=HIGHEST)
     charge_rows = jnp.broadcast_to(charges[None, None, :], (local_beads, 1, charges.shape[0]))
     packed = jnp.concatenate((first, charge_rows), axis=1)
-    force_part, unused = block_force(
-        first, charges, lax.all_gather(packed, "dom", axis=2, tiled=True)
-    )
+    force_part, unused = block_force(first, charges, gather_over(packed, "dom", 2))
     return (first, second + KICK * force_part)
 
 

time: 469 us -> 433 us (0.923)
  blocking collectives: 104 us -> 56.9 us
  starting transfers between devices: 0 us -> 11.6 us
    all_gather x1 -> x0, blocking collectives: 47 us -> none  [local(): lax.all_gather(packed, 'dom', axis=2, tiled=True)]
    all_to_all x0 -> x1, starting transfers between devices: none -> 11.6 us  [gather_over(): return jnp.concatenate(lax.all_to_all(sent, mesh_axis, 0, 0), axis=along)]
  transfers between devices with their start and end apart: 0 -> 1, of which waited for: 0 -> 0; matrix products, arithmetic and copies ran while one was open for 0% -> 0% of each run, Pallas kernels for 0% -> 0%
where the time goes in v1:
time: 433 us; the launch traced here: 432 us
  other arithmetic  274 us (63%)
  blocking collectives  56.9 us (13%)
  loops' own time  43.8 us (10%)
  local copies, waits for them, and re-layouts  43.6 us (10%)
  starting transfers between devices  11.6 us (3%)
    div x64, other arithmetic, pair_block(): near_charge[None, :, None] * far_charge[:, None, :]  108 us
    reduce_sum x64, other arithmetic, pair_block(): return (jnp.sum(terms, axis=3), -jnp.sum(terms, axis=2))  98.3 us
    reduce_sum x64, other arithmetic, pair_block(): square = jnp.sum(delta * delta, axis=1) + SOFTEN  65.7 us
    another operation x1, loops' own time, block_force(): lax.scan(one_span, jnp.zeros_like(near_pos), jnp.arange(far_count // span...  43.8 us
    dynamic_slice x64, local copies, waits for them, and re-layouts, block_force(): lax.scan(one_span, jnp.zeros_like(near_pos), jnp.arange(far_count // span...  39.5 us
    all_gather x1, blocking collectives, local(): lax.all_gather(new_vel, 'bead', axis=0, tiled=True)  28.7 us
    all_gather x1, blocking collectives, local(): lax.all_gather(new_pos, 'bead', axis=0, tiled=True)  28.3 us
    all_to_all x1, starting transfers between devices, gather_over(): return jnp.concatenate(lax.all_to_all(sent, mesh_axis, 0, 0), axis=along)  11.6 us
  transfers between devices with their start and end apart: 1, of which 0 were waited for; matrix products, arithmetic and copies ran while one was open for 0% of the time, Pallas kernels for 0%

profile of v1, /device:TPU:6, one launch (start us, length us, event | category | flops | bytes accessed | tf_op | source)
XLA Modules:
  0.0 432.3 jit_solution(1204356481395643995)
XLA Ops:
  1.7 28.3 %all_gather.6 = f32[16,3,768]{2,1,0:T(4,128)S(1)} all-gather(f32[2,3,768]{2,1,0:T(4,128)S(1)} %get-tuple-element.93), channel_id=1, replica_groups=mesh['bead'=8,'dom'=32] {'bead'}, dimensions={0}, use_global_device_ids=true | all-gather | bytes 165888 | tf_op jit(solution)/shard_map/all_gather | solution.py:88
  32.1 11.6 %all-to-all-start = ((f32[32,2,4,768]{3,2,1,0:T(4,128)}), f32[32,2,4,768]{3,2,1,0:T(4,128)S(1)}, u32[]{:S(2)}, u32[]{:S(2)}) async-start(f32[32,2,4,768]{3,2,1,0:T(4,128)} %stack.2), calls=%async_computation | async-start | bytes 1572864 | tf_op jit(solution)/shard_map/all_to_all | solution.py:17
  43.7 28.7 %all_gather.7 = f32[16,3,768]{2,1,0:T(4,128)S(1)} all-gather(f32[2,3,768]{2,1,0:T(4,128)S(1)} %get-tuple-element.92), channel_id=1, replica_groups=mesh['bead'=8,'dom'=32] {'bead'}, dimensions={0}, use_global_device_ids=true | all-gather | bytes 165888 | tf_op jit(solution)/shard_map/all_gather | solution.py:89
  73.2 358.2 %while.11 = (s32[]{:T(128)}, f32[2,3,768]{2,1,0:T(4,128)S(1)}, f32[768]{0:T(1024)S(1)}, s32[64]{0:T(128)S(1)}, f32[2,4,24576]{2,0,1:T(2,128)S(1)}, /*index=5*/f3...) while((s32[]{:T(128)}, f32[2,3,768]{2,1,0:T(4,128)S(1)}, ...), condition=%wide.region_3.4_spmd.clone, body=%wide.region_0.3_spmd.clone.sunk | while | flops 15340040 | bytes 9615561 | solution.py:77
  75.6 1.7 fusion.30
  97.9 1.7 fusion.30
  103.5 1.7 fusion.30
  109.1 1.7 fusion.30
  114.7 1.7 fusion.30
  120.3 1.7 fusion.30
  125.9 1.7 fusion.30
  131.5 1.7 fusion.30
  148.3 1.7 fusion.30
  153.9 1.7 fusion.30
  159.5 1.7 fusion.30
  165.1 1.7 fusion.30
  170.7 1.7 fusion.30
  176.3 1.7 fusion.30
  181.9 1.7 fusion.30
  204.3 1.7 fusion.30
  209.9 1.7 fusion.30
  215.5 1.7 fusion.30
  221.1 1.7 fusion.30
  226.7 1.7 fusion.30
  232.3 1.7 fusion.30
  237.9 1.7 fusion.30
  254.7 1.7 fusion.30
  260.2 1.7 fusion.30
  265.8 1.7 fusion.30
  271.4 1.7 fusion.30
  277.0 1.7 fusion.30
  282.6 1.7 fusion.30
  288.2 1.7 fusion.30
  310.6 1.7 fusion.30
  316.2 1.7 fusion.30
  321.8 1.7 fusion.30
  327.4 1.7 fusion.30
  333.0 1.7 fusion.30
  338.6 1.7 fusion.30
  344.2 1.7 fusion.30
  361.0 1.7 fusion.30
  366.6 1.7 fusion.30
  372.2 1.7 fusion.30
  377.8 1.7 fusion.30
  383.4 1.7 fusion.30
  389.0 1.7 fusion.30
  394.6 1.7 fusion.30
  417.0 1.7 fusion.30
  (491 shorter events, 245.0 us)
Async XLA Ops:
  30.3 42.9 %copy-start = (f32[2,3,768]{2,0,1:T(2,128)}, f32[2,3,768]{2,0,1:T(2,128)S(1)}, u32[]{:S(2)}) copy-start(f32[2,3,768]{2,0,1:T(2,128)S(1)} %fusion.8) | copy-start | bytes 55300
  32.1 41.2 %copy-start.1 = (f32[768]{0:T(1024)S(1)}, f32[768]{0:T(1024)}, u32[]{:S(2)}) copy-start(f32[768]{0:T(1024)} %param.7) | copy-start | bytes 9220
  32.1 40.3 %all-to-all-start = ((f32[32,2,4,768]{3,2,1,0:T(4,128)}), f32[32,2,4,768]{3,2,1,0:T(4,128)S(1)}, u32[]{:S(2)}, u32[]{:S(2)}) async-start(f32[32,2,4,768]{3,2,1,0:T(4,128)} %stack.2), calls=%async_computation | async-start | bytes 1572864 | tf_op jit(solution)/shard_map/all_to_all | solution.py:17
